TPU v7x, 32 devices: a whole 2x2x4 slice. The times are simulated.
32 devices in a mesh: row: 4 (over x, core), col: 8 (over z, y).
Axes of the slice: x: 2, y: 2, z: 4, core: 2. Of those that a mesh axis runs over, the one named last changes fastest.
Arguments:
- schur: float32 [4096, 4096], P('row', 'col'), may hold values from -6 to 6
- left_rot: float32 [8, 512, 512], P('row', 'col'), may hold values from -1 to 1, as said below
- right_rot: float32 [8, 512, 512], P('col', 'row'), may hold values from -1 to 1, as said below
- left_off: float32 [8, 512, 512], P('row', 'col'), may hold values from -1 to 1, as said below
- right_off: float32 [8, 512, 512], P('col', 'row'), may hold values from -1 to 1, as said below
Outputs:
- updated: float32 [4096, 4096], P('row', 'col')
Inputs may be any that keep to these rules, and one draw needn't show every extreme that they name: `left_rot`: each 512 x 512 block is orthogonal. `right_rot`: each 512 x 512 block is orthogonal. `left_off`: each 512 x 512 block is orthogonal. `right_off`: each 512 x 512 block is orthogonal.
All inputs are finite; a program needn't handle non-finite values.
Results may differ from a plain program's by a relative error of at most 0.00007.
Values sent between devices are 32-bit elements; how exact they have to be, the bound alone decides.
A program may use at most 64 MiB of HBM per device.

v0:
```python
import jax
import jax.numpy as jnp
from jax import lax
from jax.sharding import PartitionSpec as P


def passed_along(x, axis, by):
    size = lax.axis_size(axis)
    return lax.ppermute(x, axis, [(i, (i + by) % size) for i in range(size)])


def padded_2(cells, sides, width):
    for axis, dim in sides:
        count = lax.axis_size(axis)
        head = lax.slice_in_dim(cells, 0, width, axis=dim)
        tail = lax.slice_in_dim(cells, cells.shape[dim] - width, cells.shape[dim], axis=dim)
        cells = jnp.concatenate(
            [
                lax.ppermute(tail, axis, [(i, (i + 1) % count) for i in range(count)]),
                cells,
                lax.ppermute(head, axis, [((i + 1) % count, i) for i in range(count)]),
            ],
            axis=dim,
        )
    return cells


def apply_left(blocks, rotations):
    number = rotations.shape[0]
    window = rotations.shape[1]
    shaped = blocks.reshape(number, window, blocks.shape[1])
    result = jnp.einsum("kab,kac->kbc", rotations, shaped, precision=lax.Precision.HIGHEST)
    return result.reshape(number * window, blocks.shape[1])


def apply_right(blocks, rotations):
    number = rotations.shape[0]
    window = rotations.shape[1]
    shaped = blocks.reshape(blocks.shape[0], number, window)
    result = jnp.einsum("rka,kab->rkb", shaped, rotations, precision=lax.Precision.HIGHEST)
    return result.reshape(blocks.shape[0], number * window)


def body(schur, left_rot, right_rot, left_off, right_off):
    window = left_rot.shape[2]
    half_window = window // 2
    rows_here = schur.shape[0]
    cols_here = schur.shape[1]
    rotations = lax.all_gather(right_rot, "row", axis=1, tiled=True)
    matrix = apply_right(schur, rotations)
    rotations = lax.all_gather(left_rot, "col", axis=1, tiled=True)
    matrix = apply_left(matrix, rotations)
    rotations = lax.all_gather(right_off, "row", axis=1, tiled=True)
    following = passed_along(rotations[0][:, :half_window], "col", -1)
    padded = padded_2(matrix, (("col", 1),), half_window)
    leading = jnp.dot(
        padded[:, :window], rotations[0][:, half_window:], precision=lax.Precision.HIGHEST
    )
    middle = apply_right(padded[:, window:cols_here], rotations[1:])
    trailing = jnp.dot(
        padded[:, cols_here : cols_here + window], following, precision=lax.Precision.HIGHEST
    )
    matrix = jnp.concatenate([leading, middle, trailing], axis=1)
    rotations = lax.all_gather(left_off, "col", axis=1, tiled=True)
    following = passed_along(rotations[0][:, :half_window], "row", -1)
    padded = padded_2(matrix, (("row", 0),), half_window)
    leading = jnp.dot(
        rotations[0][:, half_window:].T, padded[:window], precision=lax.Precision.HIGHEST
    )
    middle = apply_left(padded[window:rows_here], rotations[1:])
    trailing = jnp.dot(
        following.T, padded[rows_here : rows_here + window], precision=lax.Precision.HIGHEST
    )
    return jnp.concatenate([leading, middle, trailing], axis=0)


def solution(mesh):
    return jax.shard_map(
        body,
        mesh=mesh,
        in_specs=(
            P("row", "col"),
            P("row", "col", None),
            P("col", "row", None),
            P("row", "col", None),
            P("col", "row", None),
        ),
        out_specs=P("row", "col"),
        check_vma=False,
    )
```

profile of v0, /device:TPU:1, one launch (start us, length us, event | category | flops | bytes accessed | tf_op | source)
XLA Modules:
  0.0 192.9 jit_solution(4929643086227449214)
XLA Ops:
  6.5 0.0 copy-start
  6.5 0.0 all-gather.5.cloned.1.call-start
  6.5 0.7 all-gather.5.cloned.1.call-update
  7.3 0.0 all-gather.7.cloned.1.call-start
  7.3 0.7 all-gather.7.cloned.1.call-update
  8.0 0.0 all-gather.9.cloned.1.call-start
  8.1 0.7 all-gather.9.cloned.1.call-update
  8.7 0.0 all-gather.11.cloned.1.call-start
  8.8 0.5 all-gather.11.cloned.1.call-update
  9.3 18.8 %all-gather.5.cloned.1.call-done = f32[1,512,512]{2,1,0:T(8,128)} async-done(((f32[1,128,512]{2,1,0:T(8,128)}), f32[1,512,512]{2,1,0:T(8,128)}) %all-gather.5.cloned.1.call-update) | async-done | bytes 1048592 | tf_op jit(solution)/shard_map/all_gather | solution.py:49
  28.1 0.0 copy-done
  28.1 9.3 %convolution_bitcast_fusion = f32[1024,1,512]{0,2,1:T(8,128)} fusion(f32[1024,512]{1,0:T(8,128)S(1)} %copy-done, f32[1,512,512]{2,1,0:T(8,128)} %all-gather.5.cloned.1.call-done), kind=kOutput, calls=%fused_computation.9 | convolution fusion | flops 3221225472 | bytes 5242880 | tf_op jit(solution)/shard_map/rka,kab->rkb/dot_general | solution.py:40
  37.3 3.0 %copy.7 = f32[1024,1,512]{2,0,1:T(8,128)} copy(f32[1024,1,512]{0,2,1:T(8,128)} %convolution_bitcast_fusion) | data formatting | bytes 4194304 | tf_op jit(solution)/shard_map/reshape;reshape | solution.py:31
  40.3 36.8 %all-gather.7.cloned.1.call-done = f32[2,512,512]{2,1,0:T(8,128)} async-done(((f32[2,64,512]{2,1,0:T(8,128)}), f32[2,512,512]{2,1,0:T(8,128)}) %all-gather.7.cloned.1.call-update) | async-done | bytes 2097168 | tf_op jit(solution)/shard_map/all_gather | solution.py:51
  77.1 5.8 %fusion.17 = f32[2,512,512]{1,2,0:T(8,128)S(1)} fusion(f32[2,512,512]{2,1,0:T(8,128)} %bitcast.31, f32[2,512,512]{2,1,0:T(8,128)} %all-gather.7.cloned.1.call-done), kind=kOutput, calls=%fused_computation.33 | convolution fusion | flops 3221225472 | bytes 6291456 | tf_op jit(solution)/shard_map/kab,kac->kbc/dot_general | solution.py:32
  82.8 0.0 copy-start.1
  82.8 1.4 fusion.16
  84.2 0.3 copy-done.1
  84.5 0.3 collective-permute-start
  84.8 3.9 %collective-permute-start.1 = (f32[1024,256]{1,0:T(8,128)}, f32[1024,256]{1,0:T(8,128)}, u32[]{:S(2)}, u32[]{:S(2)}) collective-permute-start(f32[1024,256]{1,0:T(8,128)} %get-tuple-element.8), channel_id=1, source_target_pairs={{1,0},{2,1},{3,2},{4,3},{5,4},{6,5},{7,6},{0,7},{9,8},{10,9},{11,1... | collective-permute-start | bytes 3145736 | tf_op jit(solution)/shard_map/ppermute | solution.py:21
  88.7 7.5 %all-gather.9.cloned.1.call-done = f32[1,512,512]{2,1,0:T(8,128)} async-done(((f32[1,128,512]{2,1,0:T(8,128)}), f32[1,512,512]{2,1,0:T(8,128)}) %all-gather.9.cloned.1.call-update) | async-done | bytes 1048592 | tf_op jit(solution)/shard_map/all_gather | solution.py:53
  96.2 1.1 slice.68
  97.3 0.0 copy-start.2
  97.3 4.2 %collective-permute-start.2 = (f32[512,256]{1,0:T(8,128)S(1)}, f32[512,256]{1,0:T(8,128)S(1)}, u32[]{:S(2)}, u32[]{:S(2)}) collective-permute-start(f32[512,256]{1,0:T(8,128)S(1)} %slice.68), channel_id=1, source_target_pairs={{0,7},{1,0},{2,1},{3,2},{4,3},{5,4},{6,5},{7,6},{8,15},{9,8},{10,9... | collective-permute-start | bytes 1572872 | tf_op jit(solution)/shard_map/ppermute | solution.py:9
  101.5 42.8 %collective-permute-done = f32[1024,256]{1,0:T(8,128)} collective-permute-done((f32[1024,256]{1,0:T(8,128)S(1)}, f32[1024,256]{1,0:T(8,128)}, u32[]{:S(2)}, u32[]{:S(2)}) %collective-permute-start) | collective-permute-done | bytes 1048608 | tf_op jit(solution)/shard_map/ppermute | solution.py:19
  144.3 3.6 %fusion.2 = f32[1024,256]{0,1:T(8,128)S(1)} fusion(f32[1024,512]{1,0:T(8,128)} %bitcast.29, f32[1024,256]{1,0:T(8,128)} %collective-permute-done, f32[512,512]{1,0:T(8,128)} %bitcast.33), kind=kOutput, calls=%fused_computation.4 | convolution fusion | flops 1611137024 | bytes 4718592 | tf_op jit(solution)/shard_map/dot_general | solution.py:56
  147.9 6.7 %collective-permute-done.2 = f32[512,256]{1,0:T(8,128)S(1)} collective-permute-done((f32[512,256]{1,0:T(8,128)S(1)}, f32[512,256]{1,0:T(8,128)S(1)}, u32[]{:S(2)}, u32[]{:S(2)}) %collective-permute-start.2) | collective-permute-done | bytes 524320 | tf_op jit(solution)/shard_map/ppermute | solution.py:9
  154.6 0.0 collective-permute-done.1
  154.6 0.0 copy-done.2
  154.6 3.3 %fusion = f32[1024,256]{0,1:T(8,128)S(1)} fusion(f32[512,256]{1,0:T(8,128)S(1)} %collective-permute-done.2, f32[1024,256]{1,0:T(8,128)} %collective-permute-done.1, f32[1024,512]{1,0:T(8,128)S(1)} %bitcast.30), kind=kOutput, calls=%fused_computation.1 | convolution fusion | flops 1611137024 | bytes 4718592 | tf_op jit(solution)/shard_map/dot_general | solution.py:60
  157.9 0.0 copy-start.3
  157.9 1.0 copy-done.3
  158.9 1.0 pad_maximum_fusion.14
  159.9 3.7 %collective-permute-start.3 = (f32[256,512]{0,1:T(8,128)}, f32[256,512]{0,1:T(8,128)}, u32[]{:S(2)}, u32[]{:S(2)}) collective-permute-start(f32[256,512]{0,1:T(8,128)} %get-tuple-element.5), channel_id=1, source_target_pairs={{0,8},{8,16},{16,24},{24,0},{1,9},{9,17},{17,25},{25,1},{2,10},{10... | collective-permute-start | bytes 1572872 | tf_op jit(solution)/shard_map/ppermute | solution.py:19
  163.6 4.1 %all-gather.11.cloned.1.call-done = f32[2,512,512]{2,1,0:T(8,128)} async-done(((f32[2,64,512]{2,1,0:T(8,128)}), f32[2,512,512]{2,1,0:T(8,128)}) %all-gather.11.cloned.1.call-update) | async-done | bytes 2097168 | tf_op jit(solution)/shard_map/all_gather | solution.py:64
  167.7 0.0 copy-start.4
  167.7 1.4 slice_bitcast_fusion.2
  169.2 1.0 collective-permute-start.5
  170.2 0.6 collective-permute-start.4
  170.8 0.0 copy-done.4
  170.8 0.0 copy-done.5
  170.9 1.9 convolution_bitcast_fusion.1
  172.7 0.0 collective-permute-done.3
  172.7 2.1 %convolution_bitcast_fusion.3 = f32[256,512]{1,0:T(8,128)S(1)} fusion(f32[256,512]{0,1:T(8,128)} %collective-permute-done.3, f32[1024,256]{0,1:T(8,128)S(1)} %copy-done.4, f32[1024,256]{0,1:T(8,128)S(1)} %fusion.2, f32[512,512]{1,0:T(8,128)S(1)} %slice_bitcast_fusion.2), kind=kOutput, calls=%fused_computation.12 | convolution fusion | flops 805830656 | bytes 3670016 | tf_op jit(solution)/shard_map/dot_general | solution.py:67
  174.9 3.3 %collective-permute-done.5 = f32[512,256]{1,0:T(8,128)S(1)} collective-permute-done((f32[512,256]{1,0:T(8,128)S(1)}, f32[512,256]{1,0:T(8,128)S(1)}, u32[]{:S(2)}, u32[]{:S(2)}) %collective-permute-start.5) | collective-permute-done | bytes 524320 | tf_op jit(solution)/shard_map/ppermute | solution.py:9
  178.2 5.6 %collective-permute-done.4 = f32[256,512]{0,1:T(8,128)S(1)} collective-permute-done((f32[256,512]{0,1:T(8,128)}, f32[256,512]{0,1:T(8,128)S(1)}, u32[]{:S(2)}, u32[]{:S(2)}) %collective-permute-start.4) | collective-permute-done | bytes 524320 | tf_op jit(solution)/shard_map/ppermute | solution.py:21
  183.8 1.1 convolution_bitcast_fusion.2
  184.9 1.5 pad_maximum_fusion.4
  (2 shorter events, 0.0 us)
Async XLA Ops:
  6.5 21.5 %copy-start = (f32[1024,512]{1,0:T(8,128)S(1)}, f32[1024,512]{1,0:T(8,128)}, u32[]{:S(2)}) copy-start(f32[1024,512]{1,0:T(8,128)} %param.5) | copy-start | bytes 6291460
  6.5 21.5 %all-gather.5.cloned.1.call-start = ((), (), s32[]{:S(2)}) async-start(), calls=%async_computation | async-start | bytes 1310720 | tf_op jit(solution)/shard_map/all_gather | solution.py:49
  7.3 69.8 %all-gather.7.cloned.1.call-start = ((), (), s32[]{:S(2)}) async-start(), calls=%async_computation.1 | async-start | bytes 2359296 | tf_op jit(solution)/shard_map/all_gather | solution.py:51
  8.0 88.2 %all-gather.9.cloned.1.call-start = ((), (), s32[]{:S(2)}) async-start(), calls=%async_computation.2 | async-start | bytes 1310720 | tf_op jit(solution)/shard_map/all_gather | solution.py:53
  8.7 159.0 %all-gather.11.cloned.1.call-start = ((), (), s32[]{:S(2)}) async-start(), calls=%async_computation.3 | async-start | bytes 2359296 | tf_op jit(solution)/shard_map/all_gather | solution.py:64
  82.8 1.7 copy-start.1
  84.5 59.8 %collective-permute-start = (f32[1024,256]{1,0:T(8,128)S(1)}, f32[1024,256]{1,0:T(8,128)}, u32[]{:S(2)}, u32[]{:S(2)}) collective-permute-start(f32[1024,256]{1,0:T(8,128)S(1)} %get-tuple-element.7), channel_id=1, source_target_pairs={{0,1},{1,2},{2,3},{3,4},{4,5},{5,6},{6,7},{7,0},{8,9},{9,10},{10,1... | collective-permute-start | bytes 3145736 | tf_op jit(solution)/shard_map/ppermute | solution.py:19
  84.8 69.9 %collective-permute-start.1 = (f32[1024,256]{1,0:T(8,128)}, f32[1024,256]{1,0:T(8,128)}, u32[]{:S(2)}, u32[]{:S(2)}) collective-permute-start(f32[1024,256]{1,0:T(8,128)} %get-tuple-element.8), channel_id=1, source_target_pairs={{1,0},{2,1},{3,2},{4,3},{5,4},{6,5},{7,6},{0,7},{9,8},{10,9},{11,1... | collective-permute-start | bytes 3145736 | tf_op jit(solution)/shard_map/ppermute | solution.py:21
  97.3 57.4 %copy-start.2 = (f32[2,512,512]{1,2,0:T(8,128)S(1)}, f32[2,512,512]{1,2,0:T(8,128)}, u32[]{:S(2)}) copy-start(f32[2,512,512]{1,2,0:T(8,128)} %copy-done.1) | copy-start | bytes 6291460
  97.3 57.3 %collective-permute-start.2 = (f32[512,256]{1,0:T(8,128)S(1)}, f32[512,256]{1,0:T(8,128)S(1)}, u32[]{:S(2)}, u32[]{:S(2)}) collective-permute-start(f32[512,256]{1,0:T(8,128)S(1)} %slice.68), channel_id=1, source_target_pairs={{0,7},{1,0},{2,1},{3,2},{4,3},{5,4},{6,5},{7,6},{8,15},{9,8},{10,9... | collective-permute-start | bytes 1572872 | tf_op jit(solution)/shard_map/ppermute | solution.py:9
  157.9 1.0 copy-start.3
  159.9 12.8 %collective-permute-start.3 = (f32[256,512]{0,1:T(8,128)}, f32[256,512]{0,1:T(8,128)}, u32[]{:S(2)}, u32[]{:S(2)}) collective-permute-start(f32[256,512]{0,1:T(8,128)} %get-tuple-element.5), channel_id=1, source_target_pairs={{0,8},{8,16},{16,24},{24,0},{1,9},{9,17},{17,25},{25,1},{2,10},{10... | collective-permute-start | bytes 1572872 | tf_op jit(solution)/shard_map/ppermute | solution.py:19
  167.7 3.1 %copy-start.4 = (f32[1024,256]{0,1:T(8,128)S(1)}, f32[1024,256]{0,1:T(8,128)}, u32[]{:S(2)}) copy-start(f32[1024,256]{0,1:T(8,128)} %copy-done.3) | copy-start | bytes 3145732
  167.7 3.1 %copy-start.5 = (f32[2,512,512]{2,1,0:T(8,128)S(1)}, f32[2,512,512]{2,1,0:T(8,128)}, u32[]{:S(2)}) copy-start(f32[2,512,512]{2,1,0:T(8,128)} %all-gather.11.cloned.1.call-done) | copy-start | bytes 6291460
  169.2 9.0 %collective-permute-start.5 = (f32[512,256]{1,0:T(8,128)S(1)}, f32[512,256]{1,0:T(8,128)S(1)}, u32[]{:S(2)}, u32[]{:S(2)}) collective-permute-start(f32[512,256]{1,0:T(8,128)S(1)} %slice.74), channel_id=1, source_target_pairs={{0,24},{8,0},{16,8},{24,16},{1,25},{9,1},{17,9},{25,17},{2,26},{10... | collective-permute-start | bytes 1572872 | tf_op jit(solution)/shard_map/ppermute | solution.py:9
  170.2 13.6 %collective-permute-start.4 = (f32[256,512]{0,1:T(8,128)}, f32[256,512]{0,1:T(8,128)S(1)}, u32[]{:S(2)}, u32[]{:S(2)}) collective-permute-start(f32[256,512]{0,1:T(8,128)} %get-tuple-element.6), channel_id=1, source_target_pairs={{8,0},{16,8},{24,16},{0,24},{9,1},{17,9},{25,17},{1,25},{10,2},{18... | collective-permute-start | bytes 1572872 | tf_op jit(solution)/shard_map/ppermute | solution.py:21
Sparse Core Ops, SparseCore 0:
  8.9 19.1 all-gather.4
  30.3 46.7 all-gather.6
  78.6 17.5 all-gather.8
  98.2 69.4 all-gather.10
where the time goes:
time: 193 us
  waiting for transfers between devices  128 us (66%)
  matrix products  27.1 us (14%)
  starting transfers between devices  13.8 us (7%)
  between operations  13.2 us (7%)
  local copies, waits for them, and re-layouts  8.15 us (4%)
  other arithmetic  2.53 us (1%)
    ppermute x2, waiting for transfers between devices, padded_2(): lax.ppermute(tail, axis, [(i, (i + 1) % count) for i in range(count)])  42.8 us
    all_gather x1, waiting for transfers between devices, body(): rotations = lax.all_gather(left_rot, 'col', axis=1, tiled=True)  36.8 us
    all_gather x1, waiting for transfers between devices, body(): rotations = lax.all_gather(right_rot, 'row', axis=1, tiled=True)  18.8 us
    ppermute x2, waiting for transfers between devices, passed_along(): return lax.ppermute(x, axis, [(i, (i + by) % size) for i in range(size)])  9.97 us
    dot_general x1, matrix products, apply_right(): jnp.einsum('rka,kab->rkb', shaped, rotations, precision=lax.Precision.HIG...  9.25 us
    dot_general x2, matrix products, apply_left(): jnp.einsum('kab,kac->kbc', rotations, shaped, precision=lax.Precision.HIG...  7.62 us
    all_gather x1, waiting for transfers between devices, body(): rotations = lax.all_gather(right_off, 'row', axis=1, tiled=True)  7.54 us
    ppermute x2, waiting for transfers between devices, padded_2(): lax.ppermute(head, axis, [((i + 1) % count, i) for i in range(count)])  5.62 us
  transfers between devices with their start and end apart: 10, of which 8 were waited for; matrix products, arithmetic and copies ran while one was open for 18% of the time, Pallas kernels for 0%

commit v1 on v0

v1 whole, which is shorter than its diff:
```python
import functools

import jax
import jax.numpy as jnp
from jax import lax
from jax.experimental import pallas as pl
from jax.experimental.pallas import tpu as pltpu
from jax.sharding import PartitionSpec as P

MESH = pl.DeviceIdType.MESH
F32 = jnp.float32
BF16 = jnp.bfloat16


def run(pred, fn):
    if pred is None:
        fn()
    else:
        pl.when(pred)(fn)


def both(a, b):
    if a is None:
        return b
    if b is None:
        return a
    return jnp.logical_and(a, b)


def split(v):
    high = v.astype(BF16)
    return high, (v - high.astype(F32)).astype(BF16)


def dot3(a, b, dims):
    def one(p, q):
        return lax.dot_general(p, q, (dims, ((), ())), preferred_element_type=F32)

    return one(a[0], b[0]) + (one(a[0], b[1]) + one(a[1], b[0]))


RIGHT = ((1,), (0,))
LEFT = ((0,), (0,))


def kernel(
    R, C, chunk,
    x, rr_in, ro_in, lr_in, lo_in, out,
    rr, ro, nx, lr, lo, nl, m, m2, m3, hp, hn, ha, hb,
    rr_h, rr_l, ro_h, ro_l, nx_h, nx_l,
    rr_s, rr_r, ro_s, ro_r, nx_s, nx_r, lr_s, lr_r, lo_s, lo_r, nl_s, nl_r,
    hp_s, hp_r, hn_s, hn_r, hr_s, hr_r,
):
    r = lax.axis_index("row")
    c = lax.axis_index("col")
    L = C // 2
    line = lax.div(c, 2)
    y = lax.rem(c, 2)
    mate = 2 * line + 1 - y
    c_next, c_prev = lax.rem(c + 1, C), lax.rem(c + C - 1, C)
    r_next, r_prev = lax.rem(r + 1, R), lax.rem(r + R - 1, R)
    can_up, can_down = line < L - 1, line > 0
    c_up, c_down = lax.rem(c + 2, C), lax.rem(c + C - 2, C)
    rows, cols = x.shape
    win = lr_in.shape[2]
    half = win // 2
    nr = rr_in.shape[0]
    nleft = lr_in.shape[0]
    pending = []

    def put(src, dst, ssem, rsem, dev, pred=None):
        def copy():
            return pltpu.make_async_remote_copy(
                src_ref=src(), dst_ref=dst(), send_sem=ssem(), recv_sem=rsem(),
                device_id=dev, device_id_type=MESH,
            )

        run(pred, lambda: copy().start())
        pending.append((pred, lambda: copy().wait_send()))

    def got(dst, rsem, pred=None):
        def wait():
            pltpu.make_async_remote_copy(
                src_ref=dst(), dst_ref=dst(), send_sem=rsem(), recv_sem=rsem(),
                device_id={"col": c_next}, device_id_type=MESH,
            ).wait_recv()

        run(pred, wait)

    barrier = pltpu.get_barrier_semaphore()

    def greet(dev, pred=None):
        run(pred, lambda: pl.semaphore_signal(barrier, inc=1, device_id=dev, device_id_type=MESH))

    for d in range(1, R):
        greet({"row": lax.rem(r + d, R)})
    greet({"col": c_next})
    greet({"col": c_prev})
    greet({"col": c_up}, can_up)
    greet({"col": c_down}, can_down)
    pl.semaphore_wait(barrier, R + 1 + can_up.astype(jnp.int32) + can_down.astype(jnp.int32))

    for d in range(1, R):
        put(lambda: rr_in, lambda: rr.at[r], lambda d=d: rr_s.at[d], lambda: rr_r.at[r],
            {"row": lax.rem(r + d, R)})

    def lr_put(src, j, k, dev, pred):
        put(src, lambda: lr.at[j], lambda: lr_s.at[k, j], lambda: lr_r.at[j], {"col": dev}, pred)

    def lo_put(src, j, k, dev, pred):
        put(src, lambda: lo.at[j], lambda: lo_s.at[k, j], lambda: lo_r.at[j], {"col": dev}, pred)

    def nl_put(src, j, pred):
        put(src, lambda: nl.at[j], lambda: nl_s.at[j], lambda: nl_r.at[j], {"row": r_prev}, pred)

    lr_put(lambda: lr_in, c, 2, mate, None)
    lr_put(lambda: lr_in, c, 0, c_up, can_up)
    lr_put(lambda: lr_in, c, 1, c_down, can_down)
    put(lambda: ro_in.at[0, :, pl.ds(0, half)], lambda: nx.at[r], lambda: nx_s.at[0],
        lambda: nx_r.at[r], {"col": c_prev})
    for d in range(1, R):
        put(lambda: ro_in, lambda: ro.at[r], lambda d=d: ro_s.at[d], lambda: ro_r.at[r],
            {"row": lax.rem(r + d, R)})
    lo_put(lambda: lo_in, c, 2, mate, None)
    lo_put(lambda: lo_in, c, 0, c_up, can_up)
    lo_put(lambda: lo_in, c, 1, c_down, can_down)
    nl_put(lambda: lo_in.at[0, :, pl.ds(0, half)], c, None)
    rr[r] = rr_in[...]
    ro[r] = ro_in[...]
    lr[c] = lr_in[...]
    lo[c] = lo_in[...]

    def lr_pass(j, k, dev, pred):
        lr_put(lambda: lr.at[j], j, k, dev, pred)

    def lr_step(s, par):
        below, above = line - 1 - s, line + 1 + s
        jb = lax.rem(2 * below + par + 2 * C, C)
        ja = lax.rem(2 * above + par, C)
        has_b, has_a = below >= 0, above <= L - 1
        got(lambda: lr.at[jb], lambda: lr_r.at[jb], has_b)
        lr_pass(jb, 0, c_up, both(has_b, can_up))
        got(lambda: lr.at[ja], lambda: lr_r.at[ja], has_a)
        lr_pass(ja, 1, c_down, both(has_a, can_down))

    def lo_step(s):
        below, above = line - 1 - s, line + 1 + s
        jb = lax.rem(2 * below + y + 2 * C, C)
        ja = lax.rem(2 * above + y, C)
        has_b, has_a = below >= 0, above <= L - 1
        for j, has, k, dev, can in (
            (jb, has_b, 0, c_up, can_up), (ja, has_a, 1, c_down, can_down),
        ):
            got(lambda: lo.at[j], lambda: lo_r.at[j], has)
            lo_put(lambda j=j: lo.at[j], j, 2, mate, has)
            lo_put(lambda j=j: lo.at[j], j, k, dev, both(has, can))
            nl_put(lambda j=j: lo.at[j, 0, :, pl.ds(0, half)], j, has)

    got(lambda: lr.at[mate], lambda: lr_r.at[mate])
    lr_pass(mate, 0, c_up, can_up)
    lr_pass(mate, 1, c_down, can_down)
    lr_step(0, y)

    for d in range(1, R):
        q = lax.rem(r + d, R)
        got(lambda: rr.at[q], lambda: rr_r.at[q])
    for w in range(nr):
        h, l = split(rr[:, w].reshape(win, win))
        rr_h[w] = h
        rr_l[w] = l
    n_chunks = rows // chunk

    def span(i):
        return pl.ds(pl.multiple_of(i * chunk, chunk), chunk)

    def halo_copies(i):
        right = pltpu.make_async_remote_copy(
            src_ref=m.at[span(i), pl.ds(cols - half, half)], dst_ref=hp.at[span(i), :],
            send_sem=hp_s.at[i], recv_sem=hp_r.at[i],
            device_id={"col": c_next}, device_id_type=MESH)
        left = pltpu.make_async_remote_copy(
            src_ref=m.at[span(i), pl.ds(0, half)], dst_ref=hn.at[span(i), :],
            send_sem=hn_s.at[i], recv_sem=hn_r.at[i],
            device_id={"col": c_prev}, device_id_type=MESH)
        return right, left

    def right_chunk(i, carry):
        for w in range(nr):
            a = split(x[span(i), pl.ds(w * win, win)])
            m[span(i), pl.ds(w * win, win)] = dot3(a, (rr_h[w], rr_l[w]), RIGHT)
        for copy in halo_copies(i):
            copy.start()
        return carry

    lax.fori_loop(0, n_chunks, right_chunk, 0)

    got(lambda: nx.at[r], lambda: nx_r.at[r])
    for d in range(1, R):
        put(lambda: nx.at[r], lambda: nx.at[r], lambda d=d: nx_s.at[d], lambda: nx_r.at[r],
            {"row": lax.rem(r + d, R)})

    lr_step(0, 1 - y)
    lo_step(0)
    for s in range(1, L - 1):
        lr_step(s, y)
        lr_step(s, 1 - y)
        lo_step(s)

    for d in range(1, R):
        q = lax.rem(r + d, R)
        got(lambda: ro.at[q], lambda: ro_r.at[q])
        got(lambda: nx.at[q], lambda: nx_r.at[q])
    for w in range(nr):
        h, l = split(ro[:, w].reshape(win, win))
        ro_h[w] = h
        ro_l[w] = l
    h, l = split(nx[...].reshape(win, half))
    nx_h[...] = h
    nx_l[...] = l

    def shifted_chunk(i, carry):
        right, left = halo_copies(i)
        right.wait_recv()
        first = split(m[span(i), pl.ds(0, half)])
        ahead = split(hp[span(i), :])
        top = (ro_h[0, :half, half:], ro_l[0, :half, half:])
        low = (ro_h[0, half:, half:], ro_l[0, half:, half:])
        m2[span(i), pl.ds(0, half)] = dot3(ahead, top, RIGHT) + dot3(first, low, RIGHT)
        for w in range(1, nr):
            a = split(m[span(i), pl.ds(w * win - half, win)])
            m2[span(i), pl.ds(w * win - half, win)] = dot3(a, (ro_h[w], ro_l[w]), RIGHT)
        left.wait_recv()
        last = split(m[span(i), pl.ds(cols - half, half)])
        after = split(hn[span(i), :])
        top = (nx_h[:half, :], nx_l[:half, :])
        low = (nx_h[half:, :], nx_l[half:, :])
        m2[span(i), pl.ds(cols - half, half)] = dot3(last, top, RIGHT) + dot3(after, low, RIGHT)
        return carry

    lax.fori_loop(0, n_chunks, shifted_chunk, 0)

    def left_window(k, carry):
        at = pl.ds(pl.multiple_of(k * win, win), win)
        q = split(lr[:, k].reshape(win, win))
        for w in range(cols // win):
            across = pl.ds(w * win, win)
            m3[at, across] = dot3(q, split(m2[at, across]), LEFT)
        return carry

    lax.fori_loop(0, nleft, left_window, 0)
    put(lambda: m3.at[pl.ds(rows - half, half), :], lambda: ha, lambda: hr_s.at[0],
        lambda: hr_r.at[0], {"row": r_next})
    put(lambda: m3.at[pl.ds(0, half), :], lambda: hb, lambda: hr_s.at[1],
        lambda: hr_r.at[1], {"row": r_prev})

    for g in range(L):
        j = 2 * g + 1 - y
        got(lambda: lo.at[j], lambda: lo_r.at[j])
        nl_put(lambda j=j: lo.at[j, 0, :, pl.ds(0, half)], j, None)

    def shifted_left(k, carry):
        at = pl.ds(pl.multiple_of(k * win - half, half), win)
        q = split(lo[:, k].reshape(win, win))
        for w in range(cols // win):
            across = pl.ds(w * win, win)
            out[at, across] = dot3(q, split(m3[at, across]), LEFT)
        return carry

    lax.fori_loop(1, nleft, shifted_left, 0)
    got(lambda: ha, lambda: hr_r.at[0])
    q = split(lo[:, 0].reshape(win, win)[:, half:])
    for w in range(cols // win):
        across = pl.ds(w * win, win)
        out[pl.ds(0, half), across] = dot3(
            (q[0][:half], q[1][:half]), split(ha[:, across]), LEFT
        ) + dot3((q[0][half:], q[1][half:]), split(m3[pl.ds(0, half), across]), LEFT)
    for j in range(C):
        got(lambda: nl.at[j], lambda: nl_r.at[j])
    got(lambda: hb, lambda: hr_r.at[1])
    q = split(nl[...].reshape(win, half))
    for w in range(cols // win):
        across = pl.ds(w * win, win)
        out[pl.ds(rows - half, half), across] = dot3(
            (q[0][:half], q[1][:half]), split(m3[pl.ds(rows - half, half), across]), LEFT
        ) + dot3((q[0][half:], q[1][half:]), split(hb[:, across]), LEFT)

    def sent(i, carry):
        for copy in halo_copies(i):
            copy.wait_send()
        return carry

    lax.fori_loop(0, n_chunks, sent, 0)
    for pred, wait in pending:
        run(pred, wait)


def solution(mesh):
    R, C = mesh.shape["row"], mesh.shape["col"]

    def body(schur, left_rot, right_rot, left_off, right_off):
        rows, cols = schur.shape
        win = left_rot.shape[2]
        half = win // 2
        nr, nleft = right_rot.shape[0], left_rot.shape[0]
        chunk = half
        n_chunks = rows // chunk
        dma = pltpu.SemaphoreType.DMA
        vm = pltpu.VMEM
        right = (R,) + right_rot.shape
        left = (C,) + left_rot.shape
        return pl.pallas_call(
            functools.partial(kernel, R, C, chunk),
            out_shape=jax.ShapeDtypeStruct((rows, cols), F32),
            in_specs=[pl.BlockSpec(memory_space=vm)] * 5,
            out_specs=pl.BlockSpec(memory_space=vm),
            scratch_shapes=[
                vm(right, F32), vm(right, F32), vm((R, win // R, half), F32),
                vm(left, F32), vm(left, F32), vm((C, win // C, half), F32),
                vm((rows, cols), F32), vm((rows, cols), F32), vm((rows, cols), F32),
                vm((rows, half), F32), vm((rows, half), F32),
                vm((half, cols), F32), vm((half, cols), F32),
                vm((nr, win, win), BF16), vm((nr, win, win), BF16),
                vm((nr, win, win), BF16), vm((nr, win, win), BF16),
                vm((win, half), BF16), vm((win, half), BF16),
                dma((R,)), dma((R,)), dma((R,)), dma((R,)), dma((R,)), dma((R,)),
                dma((3, C)), dma((C,)), dma((3, C)), dma((C,)), dma((C,)), dma((C,)),
                dma((n_chunks,)), dma((n_chunks,)), dma((n_chunks,)), dma((n_chunks,)),
                dma((2,)), dma((2,)),
            ],
            compiler_params=pltpu.CompilerParams(collective_id=0, has_side_effects=True),
        )(schur, right_rot, right_off, left_rot, left_off)

    return jax.shard_map(
        body,
        mesh=mesh,
        in_specs=(
            P("row", "col"),
            P("row", "col", None),
            P("col", "row", None),
            P("row", "col", None),
            P("col", "row", None),
        ),
        out_specs=P("row", "col"),
        check_vma=False,
    )
```

time: 193 us -> 111 us (0.58)
  waiting for transfers between devices: 128 us -> 0 us
  Pallas kernels: 0 us -> 107 us
  matrix products: 27.1 us -> 0 us
  starting transfers between devices: 13.8 us -> 0 us
  between operations: 13.2 us -> 0.01 us
  local copies, waits for them, and re-layouts: 8.15 us -> 3.08 us
  other arithmetic: 2.53 us -> 0 us
    pallas_call x0 -> x1, Pallas kernels: none -> 107 us  [body(): pl.pallas_call(functools.partial(kernel, R, C, chunk), out_shape=jax.Shap...]
    all_gather x4 -> x0, waiting for transfers between devices: 67.1 us -> none  [the longest x1 36.8 us: body(): rotations = lax.all_gather(left_rot, 'col', axis=1, tiled=True)]
    ppermute x6 -> x0, waiting for transfers between devices: 58.4 us -> none  [the longest x2 42.8 us: padded_2(): lax.ppermute(tail, axis, [(i, (i + 1) % count) for i in range(count)])]
    dot_general x7 -> x0, matrix products: 27.1 us -> none  [the longest x1 9.25 us: apply_right(): jnp.einsum('rka,kab->rkb', shaped, rotations, precision=lax.Precision.HIG...]
    ppermute x6 -> x0, starting transfers between devices: 13.7 us -> none  [the longest x2 5.21 us: passed_along(): return lax.ppermute(x, axis, [(i, (i + by) % size) for i in range(size)])]
    another operation x1 -> x0, local copies, waits for them, and re-layouts: 2.96 us -> none  [apply_left(): shaped = blocks.reshape(number, window, blocks.shape[1])]
    unnamed x4 -> x0, waiting for transfers between devices: 2.61 us -> none
    slice x3 -> x0, local copies, waits for them, and re-layouts: 2.48 us -> none  [the longest x1 1.36 us: padded_2(): lax.slice_in_dim(cells, cells.shape[dim] - width, cells.shape[dim], axis=...]
  transfers between devices with their start and end apart: 10 -> 0, of which waited for: 8 -> 0; matrix products, arithmetic and copies ran while one was open for 18% -> 0% of each run, Pallas kernels for 0% -> 0%
where the time goes in v1:
time: 111 us; the launch traced here: 110 us
  Pallas kernels  107 us (96%)
  local copies, waits for them, and re-layouts  3.08 us (3%)
    pallas_call x1, Pallas kernels, body(): pl.pallas_call(functools.partial(kernel, R, C, chunk), out_shape=jax.Shap...  107 us
    unnamed x1, local copies, waits for them, and re-layouts  3.08 us

profile of v1, /device:TPU:1, one launch (start us, length us, event | category | flops | bytes accessed | tf_op | source)
XLA Modules:
  0.0 110.4 jit_solution(9920735972400287599)
XLA Ops:
  0.0 107.3 %shard_map.55 = f32[1024,512]{1,0:T(8,128)} custom-call(f32[1024,512]{1,0:T(8,128)} %x.1, f32[1,128,512]{2,1,0:T(8,128)} %rr_in.1, f32[1,128,512]{2,1,0:T(8,128)} %ro_in.1, f32[2,64,512]{2,1,0:T(8,128)} %lr_in.1, f32[2,64,512]{2,1,0:T(8,128)} %lo_in.1), custom_call_target="tpu_custom_call" | custom-call | tf_op jit(solution)/shard_map/pallas_call | solution.py:311
  107.3 3.1 %copy.7 = f32[1024,512]{1,0:T(8,128)} copy(f32[1024,512]{1,0:T(8,128)} %shard_map.55) | data formatting | bytes 4194304

commit v2 on v1

--- a/solution.py
+++ b/solution.py
@@ -45,11 +45,11 @@
 
 def kernel(
     R, C, chunk,
-    x, rr_in, ro_in, lr_in, lo_in, out,
-    rr, ro, nx, lr, lo, nl, m, m2, m3, hp, hn, ha, hb,
+    x_in, rr_in, ro_in, lr_in, lo_in, out,
+    x, rr, ro, nx, lr, lo, nl, m, m2, m3, hp, hn, ha, hb,
     rr_h, rr_l, ro_h, ro_l, nx_h, nx_l,
     rr_s, rr_r, ro_s, ro_r, nx_s, nx_r, lr_s, lr_r, lo_s, lo_r, nl_s, nl_r,
-    hp_s, hp_r, hn_s, hn_r, hr_s, hr_r,
+    hp_s, hp_r, hn_s, hn_r, hr_s, hr_r, x_s,
 ):
     r = lax.axis_index("row")
     c = lax.axis_index("col")
@@ -67,6 +67,8 @@
     nr = rr_in.shape[0]
     nleft = lr_in.shape[0]
     pending = []
+    fetch = pltpu.make_async_copy(x_in, x, x_s)
+    fetch.start()
 
     def put(src, dst, ssem, rsem, dev, pred=None):
         def copy():
@@ -100,9 +102,25 @@
     greet({"col": c_down}, can_down)
     pl.semaphore_wait(barrier, R + 1 + can_up.astype(jnp.int32) + can_down.astype(jnp.int32))
 
-    for d in range(1, R):
-        put(lambda: rr_in, lambda: rr.at[r], lambda d=d: rr_s.at[d], lambda: rr_r.at[r],
-            {"row": lax.rem(r + d, R)})
+    peers = [lax.rem(r + 2 * d, R) for d in range(1, R // 2)]
+    sib = r + 1 - 2 * lax.rem(r, 2)
+
+    def round_rows(src, buf, ss, rs):
+        for d, q in enumerate(peers):
+            put(src, lambda: buf.at[r], lambda d=d: ss.at[d], lambda: rs.at[r], {"row": q})
+        put(src, lambda: buf.at[r], lambda: ss.at[R // 2 - 1], lambda: rs.at[r], {"row": sib})
+
+    def to_sibling(buf, ss, rs):
+        for d, q in enumerate(peers):
+            got(lambda: buf.at[q], lambda: rs.at[q])
+            put(lambda q=q: buf.at[q], lambda q=q: buf.at[q], lambda d=d: ss.at[R // 2 + d],
+                lambda q=q: rs.at[q], {"row": sib})
+
+    def from_sibling(buf, rs):
+        for q in [sib] + [lax.rem(sib + 2 * d, R) for d in range(1, R // 2)]:
+            got(lambda: buf.at[q], lambda: rs.at[q])
+
+    round_rows(lambda: rr_in, rr, rr_s, rr_r)
 
     def lr_put(src, j, k, dev, pred):
         put(src, lambda: lr.at[j], lambda: lr_s.at[k, j], lambda: lr_r.at[j], {"col": dev}, pred)
@@ -116,11 +134,9 @@
     lr_put(lambda: lr_in, c, 2, mate, None)
     lr_put(lambda: lr_in, c, 0, c_up, can_up)
     lr_put(lambda: lr_in, c, 1, c_down, can_down)
-    put(lambda: ro_in.at[0, :, pl.ds(0, half)], lambda: nx.at[r], lambda: nx_s.at[0],
+    put(lambda: ro_in.at[0, :, pl.ds(0, half)], lambda: nx.at[r], lambda: nx_s.at[R - 1],
         lambda: nx_r.at[r], {"col": c_prev})
-    for d in range(1, R):
-        put(lambda: ro_in, lambda: ro.at[r], lambda d=d: ro_s.at[d], lambda: ro_r.at[r],
-            {"row": lax.rem(r + d, R)})
+    round_rows(lambda: ro_in, ro, ro_s, ro_r)
     lo_put(lambda: lo_in, c, 2, mate, None)
     lo_put(lambda: lo_in, c, 0, c_up, can_up)
     lo_put(lambda: lo_in, c, 1, c_down, can_down)
@@ -156,14 +172,13 @@
             lo_put(lambda j=j: lo.at[j], j, k, dev, both(has, can))
             nl_put(lambda j=j: lo.at[j, 0, :, pl.ds(0, half)], j, has)
 
+    to_sibling(rr, rr_s, rr_r)
     got(lambda: lr.at[mate], lambda: lr_r.at[mate])
     lr_pass(mate, 0, c_up, can_up)
     lr_pass(mate, 1, c_down, can_down)
     lr_step(0, y)
 
-    for d in range(1, R):
-        q = lax.rem(r + d, R)
-        got(lambda: rr.at[q], lambda: rr_r.at[q])
+    from_sibling(rr, rr_r)
     for w in range(nr):
         h, l = split(rr[:, w].reshape(win, win))
         rr_h[w] = h
@@ -184,7 +199,13 @@
             device_id={"col": c_prev}, device_id_type=MESH)
         return right, left
 
+    odd = lax.rem(r, 2)
+
+    def turn(i, n):
+        return i + odd * (n - 1 - 2 * i)
+
     def right_chunk(i, carry):
+        i = turn(i, n_chunks)
         for w in range(nr):
             a = split(x[span(i), pl.ds(w * win, win)])
             m[span(i), pl.ds(w * win, win)] = dot3(a, (rr_h[w], rr_l[w]), RIGHT)
@@ -192,24 +213,22 @@
             copy.start()
         return carry
 
+    fetch.wait()
     lax.fori_loop(0, n_chunks, right_chunk, 0)
 
     got(lambda: nx.at[r], lambda: nx_r.at[r])
-    for d in range(1, R):
-        put(lambda: nx.at[r], lambda: nx.at[r], lambda d=d: nx_s.at[d], lambda: nx_r.at[r],
-            {"row": lax.rem(r + d, R)})
+    round_rows(lambda: nx.at[r], nx, nx_s, nx_r)
 
     lr_step(0, 1 - y)
+    to_sibling(ro, ro_s, ro_r)
     lo_step(0)
+    to_sibling(nx, nx_s, nx_r)
     for s in range(1, L - 1):
         lr_step(s, y)
         lr_step(s, 1 - y)
-        lo_step(s)
-
-    for d in range(1, R):
-        q = lax.rem(r + d, R)
-        got(lambda: ro.at[q], lambda: ro_r.at[q])
-        got(lambda: nx.at[q], lambda: nx_r.at[q])
+
+    from_sibling(ro, ro_r)
+    from_sibling(nx, nx_r)
     for w in range(nr):
         h, l = split(ro[:, w].reshape(win, win))
         ro_h[w] = h
@@ -219,6 +238,7 @@
     nx_l[...] = l
 
     def shifted_chunk(i, carry):
+        i = turn(i, n_chunks)
         right, left = halo_copies(i)
         right.wait_recv()
         first = split(m[span(i), pl.ds(0, half)])
@@ -237,9 +257,8 @@
         m2[span(i), pl.ds(cols - half, half)] = dot3(last, top, RIGHT) + dot3(after, low, RIGHT)
         return carry
 
-    lax.fori_loop(0, n_chunks, shifted_chunk, 0)
-
     def left_window(k, carry):
+        k = turn(k, nleft)
         at = pl.ds(pl.multiple_of(k * win, win), win)
         q = split(lr[:, k].reshape(win, win))
         for w in range(cols // win):
@@ -247,11 +266,32 @@
             m3[at, across] = dot3(q, split(m2[at, across]), LEFT)
         return carry
 
-    lax.fori_loop(0, nleft, left_window, 0)
-    put(lambda: m3.at[pl.ds(rows - half, half), :], lambda: ha, lambda: hr_s.at[0],
-        lambda: hr_r.at[0], {"row": r_next})
-    put(lambda: m3.at[pl.ds(0, half), :], lambda: hb, lambda: hr_s.at[1],
-        lambda: hr_r.at[1], {"row": r_prev})
+    def rows_up(pred):
+        put(lambda: m3.at[pl.ds(rows - half, half), :], lambda: ha, lambda: hr_s.at[0],
+            lambda: hr_r.at[0], {"row": r_next}, pred)
+
+    def rows_down(pred):
+        put(lambda: m3.at[pl.ds(0, half), :], lambda: hb, lambda: hr_s.at[1],
+            lambda: hr_r.at[1], {"row": r_prev}, pred)
+
+    per = win // chunk
+    lax.fori_loop(0, per, shifted_chunk, 0)
+    left_window(0, 0)
+    rows_down(odd == 0)
+    rows_up(odd == 1)
+    def other_windows():
+        for k in range(1, nleft):
+            lax.fori_loop(k * per, (k + 1) * per, shifted_chunk, 0)
+            left_window(k, 0)
+        rows_up(odd == 0)
+        rows_down(odd == 1)
+
+    for s in range(1, L - 1):
+        lo_step(s)
+        if s == 1:
+            other_windows()
+    if L <= 2:
+        other_windows()
 
     for g in range(L):
         j = 2 * g + 1 - y
@@ -311,10 +351,10 @@
         return pl.pallas_call(
             functools.partial(kernel, R, C, chunk),
             out_shape=jax.ShapeDtypeStruct((rows, cols), F32),
-            in_specs=[pl.BlockSpec(memory_space=vm)] * 5,
+            in_specs=[pl.BlockSpec(memory_space=pl.ANY)] + [pl.BlockSpec(memory_space=vm)] * 4,
             out_specs=pl.BlockSpec(memory_space=vm),
             scratch_shapes=[
-                vm(right, F32), vm(right, F32), vm((R, win // R, half), F32),
+                vm((rows, cols), F32), vm(right, F32), vm(right, F32), vm((R, win // R, half), F32),
                 vm(left, F32), vm(left, F32), vm((C, win // C, half), F32),
                 vm((rows, cols), F32), vm((rows, cols), F32), vm((rows, cols), F32),
                 vm((rows, half), F32), vm((rows, half), F32),
@@ -325,7 +365,7 @@
                 dma((R,)), dma((R,)), dma((R,)), dma((R,)), dma((R,)), dma((R,)),
                 dma((3, C)), dma((C,)), dma((3, C)), dma((C,)), dma((C,)), dma((C,)),
                 dma((n_chunks,)), dma((n_chunks,)), dma((n_chunks,)), dma((n_chunks,)),
-                dma((2,)), dma((2,)),
+                dma((2,)), dma((2,)), dma,
             ],
             compiler_params=pltpu.CompilerParams(collective_id=0, has_side_effects=True),
         )(schur, right_rot, right_off, left_rot, left_off)

time: 111 us -> 102 us (0.919)
  Pallas kernels: 107 us -> 99.2 us
    pallas_call x1, Pallas kernels: 107 us -> 99.2 us  [body(): pl.pallas_call(functools.partial(kernel, R, C, chunk), out_shape=jax.Shap...]
where the time goes in v2:
time: 102 us
  Pallas kernels  99.2 us (97%)
  local copies, waits for them, and re-layouts  3.08 us (3%)
    pallas_call x1, Pallas kernels, body(): pl.pallas_call(functools.partial(kernel, R, C, chunk), out_shape=jax.Shap...  99.2 us
    unnamed x1, local copies, waits for them, and re-layouts  3.08 us

profile of v2, /device:TPU:1, one launch (start us, length us, event | category | flops | bytes accessed | tf_op | source)
XLA Modules:
  0.0 102.3 jit_solution(10781046435180407471)
XLA Ops:
  0.0 99.2 %shard_map.55 = f32[1024,512]{1,0:T(8,128)} custom-call(f32[1024,512]{1,0:T(8,128)} %x_in.1, f32[1,128,512]{2,1,0:T(8,128)} %rr_in.1, f32[1,128,512]{2,1,0:T(8,128)} %ro_in.1, f32[2,64,512]{2,1,0:T(8,128)} %lr_in.1, f32[2,64,512]{2,1,0:T(8,128)} %lo_in.1), custom_call_target="tpu_custom_call" | custom-call | tf_op jit(solution)/shard_map/pallas_call | solution.py:351
  99.2 3.1 %copy.7 = f32[1024,512]{1,0:T(8,128)} copy(f32[1024,512]{1,0:T(8,128)} %shard_map.55) | data formatting | bytes 4194304

commit v3 on v2

--- a/solution.py
+++ b/solution.py
@@ -138,8 +138,6 @@
         lambda: nx_r.at[r], {"col": c_prev})
     round_rows(lambda: ro_in, ro, ro_s, ro_r)
     lo_put(lambda: lo_in, c, 2, mate, None)
-    lo_put(lambda: lo_in, c, 0, c_up, can_up)
-    lo_put(lambda: lo_in, c, 1, c_down, can_down)
     nl_put(lambda: lo_in.at[0, :, pl.ds(0, half)], c, None)
     rr[r] = rr_in[...]
     ro[r] = ro_in[...]
@@ -220,10 +218,12 @@
     round_rows(lambda: nx.at[r], nx, nx_s, nx_r)
 
     lr_step(0, 1 - y)
+    lo_put(lambda: lo_in, c, 0, c_up, can_up)
+    lo_put(lambda: lo_in, c, 1, c_down, can_down)
     to_sibling(ro, ro_s, ro_r)
     lo_step(0)
     to_sibling(nx, nx_s, nx_r)
-    for s in range(1, L - 1):
+    for s in range(1, L - 2):
         lr_step(s, y)
         lr_step(s, 1 - y)
 
@@ -257,6 +257,13 @@
         m2[span(i), pl.ds(cols - half, half)] = dot3(last, top, RIGHT) + dot3(after, low, RIGHT)
         return carry
 
+    per = win // chunk
+    lax.fori_loop(0, per, shifted_chunk, 0)
+    if L > 2:
+        lr_step(L - 2, y)
+        lo_step(1)
+        lr_step(L - 2, 1 - y)
+
     def left_window(k, carry):
         k = turn(k, nleft)
         at = pl.ds(pl.multiple_of(k * win, win), win)
@@ -274,8 +281,6 @@
         put(lambda: m3.at[pl.ds(0, half), :], lambda: hb, lambda: hr_s.at[1],
             lambda: hr_r.at[1], {"row": r_prev}, pred)
 
-    per = win // chunk
-    lax.fori_loop(0, per, shifted_chunk, 0)
     left_window(0, 0)
     rows_down(odd == 0)
     rows_up(odd == 1)
@@ -286,43 +291,58 @@
         rows_up(odd == 0)
         rows_down(odd == 1)
 
-    for s in range(1, L - 1):
+    other_windows()
+    for s in range(2, L - 1):
         lo_step(s)
-        if s == 1:
-            other_windows()
-    if L <= 2:
-        other_windows()
-
+
+    strip = win // C
+
+    def stack(ref, at, par):
+        return jnp.concatenate(
+            [ref[pl.ds(pl.multiple_of(at + (2 * g + par) * strip, strip), strip), :]
+             for g in range(L // 2)], axis=0)
+
+    def product(q, parts, at, add):
+        b = split(jnp.concatenate(parts, axis=0))
+        res = dot3(split(q), b, LEFT)
+        out[at, :] = out[at, :] + res if add else res
+
+    def off(k, par, lo_cut, hi_cut):
+        return jnp.concatenate([lo[2 * g + par, k, :, lo_cut:hi_cut] for g in range(L)], axis=0)
+
+    def middle(par, add):
+        for k in range(1, nleft):
+            base = k * win - half
+            product(off(k, par, 0, win),
+                    [stack(m3, base, par), stack(m3, k * win, par)], pl.ds(base, win), add)
+
+    def leading(par, add):
+        product(off(0, par, half, win),
+                [stack(ha, 0, par), stack(m3, 0, par)], pl.ds(0, half), add)
+
+    def trailing(par, add):
+        q = jnp.concatenate([nl[2 * g + par] for g in range(L)], axis=0)
+        product(q, [stack(m3, rows - half, par), stack(hb, 0, par)],
+                pl.ds(rows - half, half), add)
+
+    middle(y, False)
+    got(lambda: ha, lambda: hr_r.at[0])
+    leading(y, False)
+    for g in range(L):
+        j = 2 * g + y
+        got(lambda: nl.at[j], lambda: nl_r.at[j])
+    got(lambda: hb, lambda: hr_r.at[1])
+    trailing(y, False)
     for g in range(L):
         j = 2 * g + 1 - y
         got(lambda: lo.at[j], lambda: lo_r.at[j])
         nl_put(lambda j=j: lo.at[j, 0, :, pl.ds(0, half)], j, None)
-
-    def shifted_left(k, carry):
-        at = pl.ds(pl.multiple_of(k * win - half, half), win)
-        q = split(lo[:, k].reshape(win, win))
-        for w in range(cols // win):
-            across = pl.ds(w * win, win)
-            out[at, across] = dot3(q, split(m3[at, across]), LEFT)
-        return carry
-
-    lax.fori_loop(1, nleft, shifted_left, 0)
-    got(lambda: ha, lambda: hr_r.at[0])
-    q = split(lo[:, 0].reshape(win, win)[:, half:])
-    for w in range(cols // win):
-        across = pl.ds(w * win, win)
-        out[pl.ds(0, half), across] = dot3(
-            (q[0][:half], q[1][:half]), split(ha[:, across]), LEFT
-        ) + dot3((q[0][half:], q[1][half:]), split(m3[pl.ds(0, half), across]), LEFT)
-    for j in range(C):
+    middle(1 - y, True)
+    leading(1 - y, True)
+    for g in range(L):
+        j = 2 * g + 1 - y
         got(lambda: nl.at[j], lambda: nl_r.at[j])
-    got(lambda: hb, lambda: hr_r.at[1])
-    q = split(nl[...].reshape(win, half))
-    for w in range(cols // win):
-        across = pl.ds(w * win, win)
-        out[pl.ds(rows - half, half), across] = dot3(
-            (q[0][:half], q[1][:half]), split(m3[pl.ds(rows - half, half), across]), LEFT
-        ) + dot3((q[0][half:], q[1][half:]), split(hb[:, across]), LEFT)
+    trailing(1 - y, True)
 
     def sent(i, carry):
         for copy in halo_copies(i):

time: 102 us -> 99.5 us (0.975)
  Pallas kernels: 99.2 us -> 96.3 us
    pallas_call x1, Pallas kernels: 99.2 us -> 96.3 us  [body(): pl.pallas_call(functools.partial(kernel, R, C, chunk), out_shape=jax.Shap...]
where the time goes in v3:
time: 99.5 us; the launch traced here: 99.4 us
  Pallas kernels  96.3 us (97%)
  local copies, waits for them, and re-layouts  3.08 us (3%)
    pallas_call x1, Pallas kernels, body(): pl.pallas_call(functools.partial(kernel, R, C, chunk), out_shape=jax.Shap...  96.3 us
    unnamed x1, local copies, waits for them, and re-layouts  3.08 us

profile of v3, /device:TPU:1, one launch (start us, length us, event | category | flops | bytes accessed | tf_op | source)
XLA Modules:
  0.0 99.4 jit_solution(310318857101131932)
XLA Ops:
  0.0 96.3 %shard_map.55 = f32[1024,512]{1,0:T(8,128)} custom-call(f32[1024,512]{1,0:T(8,128)} %x_in.1, f32[1,128,512]{2,1,0:T(8,128)} %rr_in.1, f32[1,128,512]{2,1,0:T(8,128)} %ro_in.1, f32[2,64,512]{2,1,0:T(8,128)} %lr_in.1, f32[2,64,512]{2,1,0:T(8,128)} %lo_in.1), custom_call_target="tpu_custom_call" | custom-call | tf_op jit(solution)/shard_map/pallas_call | solution.py:371
  96.3 3.1 %copy.7 = f32[1024,512]{1,0:T(8,128)} copy(f32[1024,512]{1,0:T(8,128)} %shard_map.55) | data formatting | bytes 4194304
